TPU v7x, 32 devices: a whole 2x2x4 slice. The times are simulated.
32 devices in a mesh: frow: 4 (over y, x), fcol: 2 (over core), sub: 4 (over z).
Axes of the slice: x: 2, y: 2, z: 4, core: 2. Of those that a mesh axis runs over, the one named last changes fastest.
Arguments:
- contrib: bfloat16 [4, 8192, 4096], P('sub', 'frow', 'fcol'), may hold values from -6 to 6, as said below
- row_map: int32 [4, 16], replicated, may hold values from -1 to 63, as said below
- front_slot: int32 [64], replicated, may hold values from 0 to 63, as said below
- own_diag: float32 [32768], P('frow'), may hold values from 128 to 256
- pattern: int32 [64, 8], P('frow', ('fcol', 'sub')), may hold values 0 or 1
Outputs:
- window: float32 [32768, 4096], P('frow', ('fcol', 'sub'))
Inputs may be any that keep to these rules, and one draw needn't show every extreme that they name: `contrib`: each child's contribution entries. `front_slot`: A permutation of 0 to 63. `row_map`: each child's live rows come first and number 16 - 1 to 16, some child having all 16 live; a child's live entries are distinct; every child has a live row that maps to front block row 0; live row f * 4 + g + m (0 <= m < 1) of a child goes to a front row i with front_slot[i] // 16 = g.
All inputs are finite; a program needn't handle non-finite values. No bound on the sum of `pattern` on one device may be relied on, other than what follows from the above.
Results may differ from a plain program's by a relative error of at most 0.0025.
Values may be sent and summed in bfloat16 or wider, within the bound.
No kernel may reach another device: no remote copies, remote signals or barrier semaphores. Data moves between devices by JAX's collectives and lax.ppermute only.
A program may use at most 192 MiB of HBM per device.

v0:
```python
import jax
import jax.numpy as jnp
from jax import lax
from jax.sharding import PartitionSpec as P

BLK = 512
FB = 64


def from_root(block, axis, source):
    block = jnp.where(lax.axis_index(axis) == source, block, jnp.zeros_like(block))
    return lax.psum(block, axis)


def on_device(contrib, row_map, front_slot, own_diag, pattern):
    owner_count = lax.axis_size("frow")
    child_count = lax.axis_size("sub")
    owner_blocks = FB // owner_count
    row_index = lax.axis_index("frow")
    column = lax.axis_index(("fcol", "sub"))
    local_rows = contrib.shape[1] // BLK
    per_owner = local_rows // owner_count
    pieces = contrib[0].reshape(owner_count, per_owner, BLK, child_count, BLK)
    grouped_map = row_map.reshape(child_count, owner_count, owner_count, per_owner)
    here_map = lax.dynamic_index_in_dim(grouped_map, row_index, 2, keepdims=False)
    here_map = jnp.transpose(here_map, (1, 2, 0))
    live_here = here_map >= 0
    stored_here = front_slot[jnp.maximum(here_map, 0)]
    matches = live_here & (stored_here // owner_blocks == row_index)
    position_here = stored_here - row_index * owner_blocks
    local_slots = jnp.arange(owner_blocks)[:, None, None, None]
    assignment = jnp.where(matches[None] & (position_here[None] == local_slots), 1.0, 0.0).astype(
        jnp.bfloat16
    )
    received = lax.all_to_all(
        lax.all_to_all(pieces, "frow", split_axis=0, concat_axis=0, tiled=True),
        "sub",
        split_axis=3,
        concat_axis=3,
        tiled=True,
    )
    blocks = jnp.einsum("qfmc,fmacb->qab", assignment, received, preferred_element_type=jnp.float32)
    home_slot = front_slot[column]
    owns_home = home_slot // owner_blocks == row_index
    position = jnp.clip(home_slot - row_index * owner_blocks, 0, owner_blocks - 1)
    values = lax.dynamic_index_in_dim(
        own_diag.reshape(owner_blocks, BLK), position, 0, keepdims=False
    )
    diagonal_add = jnp.diag(values) * jnp.where(owns_home, 1.0, 0.0)
    current = lax.dynamic_index_in_dim(blocks, position, 0, keepdims=False)
    assembled = lax.dynamic_update_index_in_dim(blocks, current + diagonal_add, position, 0)
    home_slot = front_slot[0]
    root_row = home_slot // owner_blocks
    position = home_slot % owner_blocks
    diagonal = lax.dynamic_index_in_dim(assembled, position, 0, keepdims=False)
    diagonal = from_root(diagonal.astype(jnp.bfloat16), "frow", root_row).astype(diagonal.dtype)
    symmetric = 0.5 * (diagonal + diagonal.T)
    cholesky_factor = jnp.linalg.cholesky(symmetric)
    identity = jnp.eye(BLK, dtype=jnp.float32)
    inverse = lax.linalg.triangular_solve(cholesky_factor, identity, left_side=True, lower=True)
    panel = jnp.dot(
        assembled.reshape(-1, BLK),
        inverse.T,
        precision=lax.Precision.HIGHEST,
        preferred_element_type=jnp.float32,
    )
    shared = from_root(panel.astype(jnp.bfloat16), ("fcol", "sub"), 0)
    home_slot = front_slot[column]
    root_row = home_slot // owner_blocks
    position = home_slot % owner_blocks
    column_piece = lax.dynamic_index_in_dim(
        shared.reshape(owner_blocks, BLK, BLK), position, 0, keepdims=False
    )
    column_piece = from_root(column_piece, "frow", root_row)
    update = jnp.einsum("ra,ba->rb", shared, column_piece, preferred_element_type=jnp.float32)
    pattern_gate = pattern[:, 0].astype(jnp.float32)
    trailing = (
        assembled - pattern_gate[:, None, None] * update.reshape(owner_blocks, BLK, BLK)
    ).reshape(-1, BLK)
    return jnp.where(column == 0, panel, trailing)


def solution(mesh):
    return jax.shard_map(
        on_device,
        mesh=mesh,
        in_specs=(P("sub", "frow", "fcol"), P(), P(), P("frow"), P("frow", ("fcol", "sub"))),
        out_specs=P("frow", ("fcol", "sub")),
        check_vma=False,
    )
```

profile of v0, /device:TPU:0, one launch (start us, length us, event | category | flops | bytes accessed | tf_op | source)
XLA Modules:
  0.0 899.4 jit_solution(4407061158511109020)
XLA Ops:
  6.5 14.5 %reshape_squeeze.3 = bf16[4,1,512,4,512]{4,3,2,0,1:T(4,128)(2,1)} reshape(bf16[1,2048,2048]{2,1,0:T(8,128)(2,1)} %param.5) | data formatting | bytes 16777216 | tf_op jit(solution)/shard_map/reshape;squeeze | solution.py:23
  21.0 98.5 %all_to_all.10 = bf16[4,1,512,4,512]{4,3,2,1,0:T(4,128)(2,1)S(1)} all-to-all(bf16[4,1,512,4,512]{4,3,2,1,0:T(4,128)(2,1)} %bitcast.96), channel_id=1, replica_groups=mesh['frow'=4,'fcol'=2,'sub'=4] {'frow'}, dimensions={0} | all-to-all | bytes 16777216 | tf_op jit(solution)/shard_map/all_to_all | solution.py:36
  119.5 20.9 %copy.44 = bf16[4,1,512,4,512]{4,0,2,1,3:T(4,128)(2,1)} copy(bf16[4,1,512,4,512]{4,3,2,1,0:T(4,128)(2,1)S(1)} %all_to_all.10) | data formatting | bytes 16777216 | tf_op jit(solution)/shard_map/all_to_all | solution.py:36
  140.4 5.7 all-to-all-start.1
  146.1 0.6 fusion.59
  151.6 0.2 maximum_reduce_fusion
  152.0 0.7 gather_fusion
  153.7 0.2 compare_reduce_fusion
  153.9 174.5 %all-to-all-done.1 = bf16[4,1,512,4,512]{4,0,2,1,3:T(4,128)(2,1)} async-done(((bf16[4,1,512,4,512]{4,0,2,1,3:T(4,128)(2,1)}), bf16[4,1,512,4,512]{4,0,2,1,3:T(4,128)(2,1)}, u32[]{:S(2)}, u32[]{:S(2)}) %all-to-all-start.1) | async-done | bytes 8388640 | tf_op jit(solution)/shard_map/all_to_all | solution.py:35
  328.4 11.5 %convolution_bitcast_fusion = f32[16,512,512]{2,0,1:T(8,128)} fusion(bf16[4,1,512,4,512]{4,0,2,1,3:T(4,128)(2,1)} %all-to-all-done.1, s32[4,4]{0,1:T(4,128)S(1)} %copy.42, pred[4,4]{0,1:T(4,128)(4,1)S(1)} %fusion.52), kind=kOutput, calls=%fused_computation.5 | convolution fusion | flops 134218752 | bytes 25165904 | tf_op jit(solution)/shard_map/qfmc,fmacb->qab/dot_general | solution.py:42
  339.9 19.3 %copy.47 = f32[16,512,512]{1,2,0:T(8,128)} copy(f32[16,512,512]{2,0,1:T(8,128)} %convolution_bitcast_fusion) | data formatting | bytes 33554432 | tf_op jit(solution)/shard_map/qfmc,fmacb->qab/dot_general | solution.py:42
  359.2 2.4 add_dynamic-update-slice_fusion
  361.5 2.1 fusion.18
  363.9 17.8 %copy.48 = f32[16,512,512]{2,1,0:T(8,128)} copy(f32[16,512,512]{1,2,0:T(8,128)} %add_dynamic-update-slice_fusion) | data formatting | bytes 33554432 | tf_op jit(solution)/shard_map/jit(dynamic_update_index_in_dim)/dynamic_update_slice | solution.py:51
  381.7 25.4 %all-reduce.5.cloned.1.call-done = bf16[512,512]{0,1:T(8,128)(2,1)} async-done(((bf16[512,512]{0,1:T(8,128)(2,1)}), bf16[512,512]{0,1:T(8,128)(2,1)}) %all-reduce.5.cloned.1.call-update) | async-done | bytes 524304 | tf_op jit(solution)/shard_map/psum | solution.py:12
  407.1 1.3 copy.49
  408.4 1.2 fusion.11
  409.6 0.3 copy.50
  409.9 0.2 fusion.10
  410.1 1.0 copy-done.1
  411.1 11.7 %cholesky.103 = f32[128,128]{1,0:T(8,128)S(1)} custom-call(f32[128,128]{1,0:T(8,128)S(1)} %cholesky.263), custom_call_target="Cholesky" | custom-call | tf_op jit(solution)/shard_map/jit(cholesky)/cholesky | solution.py:58
  423.0 9.8 %custom-call.30 = f32[1,128,128]{1,2,0:T(8,128)S(1)} custom-call(f32[1,128,128]{2,1,0:T(8,128)S(1)} %get-tuple-element.32), custom_call_target="InvertDiagBlocksLowerTriangular" | custom-call | tf_op jit(solution)/shard_map/jit(cholesky)/cholesky | solution.py:58
  432.8 1.2 constant_dynamic-update-slice_fusion
  434.1 1.3 convolution_subtract_fusion.3
  435.4 11.7 %cholesky.215 = f32[128,128]{1,0:T(8,128)S(1)} custom-call(f32[128,128]{1,0:T(8,128)S(1)} %cholesky.267), custom_call_target="Cholesky" | custom-call | tf_op jit(solution)/shard_map/jit(cholesky)/cholesky | solution.py:58
  447.1 10.0 %custom-call.31 = f32[1,128,128]{1,2,0:T(8,128)S(1)} custom-call(f32[1,128,128]{2,1,0:T(8,128)S(1)} %get-tuple-element.29), custom_call_target="InvertDiagBlocksLowerTriangular" | custom-call | tf_op jit(solution)/shard_map/jit(cholesky)/cholesky | solution.py:58
  457.1 0.3 convolution_dynamic-update-slice_fusion
  457.4 1.3 convolution_subtract_fusion.4
  458.7 11.7 %cholesky.236 = f32[128,128]{1,0:T(8,128)S(1)} custom-call(f32[128,128]{1,0:T(8,128)S(1)} %cholesky.272), custom_call_target="Cholesky" | custom-call | tf_op jit(solution)/shard_map/jit(cholesky)/cholesky | solution.py:58
  470.4 9.8 %custom-call.32 = f32[1,128,128]{1,2,0:T(8,128)S(1)} custom-call(f32[1,128,128]{2,1,0:T(8,128)S(1)} %get-tuple-element.26), custom_call_target="InvertDiagBlocksLowerTriangular" | custom-call | tf_op jit(solution)/shard_map/jit(cholesky)/cholesky | solution.py:58
  480.4 1.2 convolution_subtract_fusion.5
  481.7 12.1 %cholesky.253 = f32[128,128]{1,0:T(8,128)S(1)} custom-call(f32[128,128]{1,0:T(8,128)S(1)} %convolution_subtract_fusion.5), custom_call_target="Cholesky" | custom-call | tf_op jit(solution)/shard_map/jit(cholesky)/cholesky | solution.py:58
  493.8 0.7 compare_reduce_fusion.2
  494.5 0.6 compare_reduce_fusion.1
  495.1 0.7 compare_reduce_fusion.3
  498.5 10.5 %while.1 = (s32[]{:T(128)}, f32[512,512]{1,0:T(8,128)S(1)}, s32[4,2]{0,1:T(2,128)S(1)}, f32[4,128,128]{2,1,0:T(8,128)}, s32[]{:T(128)}) while((s32[]{:T(128)}, f32[512,512]{1,0:T(8,128)S(1)}, s32[4,2]{0,1:T(2,128)S(1)}, f32[4,128,128]{2,1,0:T(8,128)}, s32[]{:T(128)}) %tuple.29), condition=%wide.while_cond, body=%wide.while_body.sunk | while | flops 2 | bytes 132205 | solution.py:60
  498.6 0.6 fusion.70
  499.2 2.0 bitcast_dynamic-update-slice_fusion.2
  501.2 0.6 fusion.70
  501.8 2.0 bitcast_dynamic-update-slice_fusion.2
  503.9 0.6 fusion.70
  504.5 2.0 bitcast_dynamic-update-slice_fusion.2
  506.5 0.6 fusion.70
  507.1 2.0 bitcast_dynamic-update-slice_fusion.2
  509.1 40.1 %custom-call.33 = f32[4,128,128]{1,2,0:T(8,128)S(1)} custom-call(f32[4,128,128]{2,1,0:T(8,128)} %get-tuple-element.12), custom_call_target="InvertDiagBlocksLowerTriangular" | custom-call | tf_op jit(solution)/shard_map/triangular_solve | solution.py:60
  549.2 0.3 fusion.24
  549.5 0.4 convolution_subtract_fusion.1
  549.9 0.4 fusion.36
  550.3 0.4 convolution_subtract_fusion
  550.8 0.4 fusion.34
  551.2 0.6 convolution_subtract_fusion.2
  551.8 0.4 fusion.33
  552.3 31.9 %convert_select_fusion = (bf16[8192,512]{1,0:T(8,128)(2,1)}, f32[8192,512]{1,0:T(8,128)}) fusion(pred[]{:T(512)S(6)} %eq.66, f32[8192,512]{1,0:T(8,128)} %bitcast.94, f32[128,512]{1,0:T(8,128)S(1)} %fusion.33, f32[128,512]{1,0:T(8,128)S(1)} %fusion.34, f32[128,512]{1,0:T(8,128)S(1)} %fusion.36, f32[128,512]{1,0:T(8,128)S(1)} %fusion.24), kind=kOutput, calls=%fused_computation.8 | convolution fusion | flops 25778978816 | bytes 42991616 | tf_op jit(solution)/shard_map/dot_general | solution.py:61
  584.2 0.2 all-reduce.9.cloned.1.call-start
  584.4 175.4 %all-reduce.7.cloned.1.call-done = bf16[8192,512]{1,0:T(8,128)(2,1)} async-done(((bf16[8192,512]{1,0:T(8,128)(2,1)}), bf16[8192,512]{1,0:T(8,128)(2,1)}) %all-reduce.7.cloned.1.call-update) | async-done | bytes 8388624 | tf_op jit(solution)/shard_map/psum | solution.py:12
  759.9 1.1 constant_dynamic-slice_fusion.1
  760.9 0.2 copy.56
  761.2 0.8 select_bitcast_fusion
  762.0 46.3 %all-reduce.9.cloned.1.call-done = bf16[512,512]{0,1:T(8,128)(2,1)} async-done(((bf16[512,512]{0,1:T(8,128)(2,1)}), bf16[512,512]{0,1:T(8,128)(2,1)}) %all-reduce.9.cloned.1.call-update) | async-done | bytes 524304 | tf_op jit(solution)/shard_map/psum | solution.py:12
  808.4 14.1 %fusion.60 = f32[8192,512]{1,0:T(8,128)} fusion(bf16[8192,512]{1,0:T(8,128)(2,1)} %all-reduce.7.cloned.1.call-done, bf16[512,512]{0,1:T(8,128)(2,1)} %all-reduce.9.cloned.1.call-done), kind=kOutput, calls=%fused_computation.120 | convolution fusion | flops 4294967296 | bytes 25690112 | tf_op jit(solution)/shard_map/ra,ba->rb/dot_general | solution.py:75
  822.5 17.6 %copy.52 = f32[16,512,512]{1,2,0:T(8,128)} copy(f32[16,512,512]{2,1,0:T(8,128)} %bitcast.95) | data formatting | bytes 33554432 | tf_op jit(solution)/shard_map/reshape | solution.py:78
  840.1 17.4 %multiply_subtract_fusion = f32[16,512,512]{1,2,0:T(8,128)} fusion(f32[16,512,512]{1,2,0:T(8,128)} %add_dynamic-update-slice_fusion, f32[16,512,512]{1,2,0:T(8,128)} %copy.52, f32[16]{0:T(128)S(1)} %convert_bitcast_fusion), kind=kLoop, calls=%fused_computation.4 | loop fusion | flops 8388608 | bytes 50331712 | tf_op jit(solution)/shard_map/sub | solution.py:78
  857.5 17.6 %copy.53 = f32[16,512,512]{2,1,0:T(8,128)} copy(f32[16,512,512]{1,2,0:T(8,128)} %multiply_subtract_fusion) | data formatting | bytes 33554432 | tf_op jit(solution)/shard_map/sub | solution.py:78
  875.1 17.6 %bitcast_select_fusion = f32[8192,512]{1,0:T(8,128)} fusion(f32[8192,512]{1,0:T(8,128)} %get-tuple-element.38, f32[16,512,512]{2,1,0:T(8,128)} %copy.53, pred[]{:T(512)S(6)} %eq.66), kind=kLoop, calls=%fused_computation.3 | loop fusion | flops 4194304 | bytes 50331648 | tf_op jit(solution)/shard_map/jit(_where)/select_n | solution.py:80
  (45 shorter events, 1.8 us)
Async XLA Ops:
  119.5 26.6 %copy-start = (s32[64]{0:T(128)S(1)}, s32[64]{0:T(128)}, u32[]{:S(2)}) copy-start(s32[64]{0:T(128)} %param.7) | copy-start | bytes 772
  119.5 32.0 %copy-start.3 = (s32[4,16]{1,0:T(4,128)S(1)}, s32[4,16]{1,0:T(4,128)}, u32[]{:S(2)}) copy-start(s32[4,16]{1,0:T(4,128)} %param.6) | copy-start | bytes 772
  119.5 34.1 %copy-start.2 = (f32[8192]{0:T(1024)S(1)}, f32[8192]{0:T(1024)}, u32[]{:S(2)}) copy-start(f32[8192]{0:T(1024)} %param.8) | copy-start | bytes 98308
  140.4 188.0 %all-to-all-start.1 = ((bf16[4,1,512,4,512]{4,0,2,1,3:T(4,128)(2,1)}), bf16[4,1,512,4,512]{4,0,2,1,3:T(4,128)(2,1)}, u32[]{:S(2)}, u32[]{:S(2)}) async-start(bf16[4,1,512,4,512]{4,0,2,1,3:T(4,128)(2,1)} %copy.44), calls=%async_computation.1 | async-start | bytes 16777216 | tf_op jit(solution)/shard_map/all_to_all | solution.py:35
  146.0 261.1 %all-reduce.5.cloned.1.call-start = ((), (), s32[]{:S(2)}) async-start(), calls=%async_computation.2 | async-start | bytes 1048576 | tf_op jit(solution)/shard_map/psum | solution.py:12
  363.6 396.2 %all-reduce.7.cloned.1.call-start = ((), (), s32[]{:S(2)}) async-start(), calls=%async_computation.3 | async-start | bytes 16777216 | tf_op jit(solution)/shard_map/psum | solution.py:12
  410.1 1.0 copy-start.1
  552.3 209.8 %copy-start.4 = (s32[16,1]{0,1:T(1,128)S(1)}, s32[16,1]{0,1:T(1,128)}, u32[]{:S(2)}) copy-start(s32[16,1]{0,1:T(1,128)} %param.9) | copy-start | bytes 196
  584.2 224.2 %all-reduce.9.cloned.1.call-start = ((), (), s32[]{:S(2)}) async-start(), calls=%async_computation.4 | async-start | bytes 1048576 | tf_op jit(solution)/shard_map/psum | solution.py:12
Sparse Core Ops, SparseCore 0:
  363.8 43.2 all-reduce.4
  584.3 175.5 all-reduce.6
  762.9 45.4 all-reduce.8
where the time goes:
time: 907 us; the launch traced here: 899 us
  waiting for transfers between devices  422 us (47%)
  other arithmetic  162 us (18%)
  local copies, waits for them, and re-layouts  124 us (14%)
  blocking collectives  98.5 us (11%)
  matrix products  66 us (7%)
  between operations  21.7 us (2%)
    psum x3, waiting for transfers between devices, from_root(): return lax.psum(block, axis)  247 us
    all_to_all x1, waiting for transfers between devices, on_device(): lax.all_to_all(lax.all_to_all(pieces, 'frow', split_axis=0, concat_axis=0...  174 us
    all_to_all x1, blocking collectives, on_device(): lax.all_to_all(pieces, 'frow', split_axis=0, concat_axis=0, tiled=True)  98.5 us
    another operation x14, other arithmetic, on_device(): cholesky_factor = jnp.linalg.cholesky(symmetric)  79 us
    another operation x3, other arithmetic, on_device(): lax.linalg.triangular_solve(cholesky_factor, identity, left_side=True, lo...  40.3 us
    dot_general x1, matrix products, on_device(): jnp.dot(assembled.reshape(-1, BLK), inverse.T, precision=lax.Precision.HI...  31.9 us
    all_to_all x1, local copies, waits for them, and re-layouts, on_device(): lax.all_to_all(pieces, 'frow', split_axis=0, concat_axis=0, tiled=True)  20.9 us
    dot_general x1, local copies, waits for them, and re-layouts, on_device(): jnp.einsum('qfmc,fmacb->qab', assignment, received, preferred_element_typ...  19.3 us
  transfers between devices with their start and end apart: 4, of which 4 were waited for; matrix products, arithmetic and copies ran while one was open for 2% of the time, Pallas kernels for 0%

commit v1 on v0

--- a/solution.py
+++ b/solution.py
@@ -9,7 +9,7 @@
 
 def from_root(block, axis, source):
     block = jnp.where(lax.axis_index(axis) == source, block, jnp.zeros_like(block))
-    return lax.psum(block, axis)
+    return jnp.sum(lax.all_gather(block, axis), axis=0)
 
 
 def on_device(contrib, row_map, front_slot, own_diag, pattern):

time: 907 us -> 1290 us (1.42)
  waiting for transfers between devices: 422 us -> 786 us
  other arithmetic: 162 us -> 176 us
    all_gather x0 -> x3, waiting for transfers between devices: none -> 612 us  [from_root(): return jnp.sum(lax.all_gather(block, axis), axis=0)]
    psum x3 -> x0, waiting for transfers between devices: 247 us -> none  [from_root(): return lax.psum(block, axis)]
    reduce_sum x0 -> x3, other arithmetic: none -> 30.2 us  [from_root(): return jnp.sum(lax.all_gather(block, axis), axis=0)]
    dynamic_update_slice x1 -> x2, local copies, waits for them, and re-layouts: 17.8 us -> 39.4 us  [on_device(): lax.dynamic_update_index_in_dim(blocks, current + diagonal_add, position, 0)]
    reshape x1 -> x0, local copies, waits for them, and re-layouts: 17.6 us -> none  [on_device(): update.reshape(owner_blocks, BLK, BLK)]
    sub x1 -> x0, other arithmetic: 17.4 us -> none  [on_device(): assembled - pattern_gate[:, None, None] * update.reshape(owner_blocks, BL...]
where the time goes in v1:
time: 1290 us; the launch traced here: 1280 us
  waiting for transfers between devices  786 us (61%)
  other arithmetic  176 us (14%)
  local copies, waits for them, and re-layouts  118 us (9%)
  blocking collectives  98.5 us (8%)
  matrix products  74.2 us (6%)
  between operations  21.6 us (2%)
    all_gather x3, waiting for transfers between devices, from_root(): return jnp.sum(lax.all_gather(block, axis), axis=0)  612 us
    all_to_all x1, waiting for transfers between devices, on_device(): lax.all_to_all(lax.all_to_all(pieces, 'frow', split_axis=0, concat_axis=0...  174 us
    all_to_all x1, blocking collectives, on_device(): lax.all_to_all(pieces, 'frow', split_axis=0, concat_axis=0, tiled=True)  98.5 us
    another operation x14, other arithmetic, on_device(): cholesky_factor = jnp.linalg.cholesky(symmetric)  78.7 us
    another operation x3, other arithmetic, on_device(): lax.linalg.triangular_solve(cholesky_factor, identity, left_side=True, lo...  40.4 us
    dynamic_update_slice x2, local copies, waits for them, and re-layouts, on_device(): lax.dynamic_update_index_in_dim(blocks, current + diagonal_add, position, 0)  39.4 us
    dot_general x1, matrix products, on_device(): jnp.dot(assembled.reshape(-1, BLK), inverse.T, precision=lax.Precision.HI...  31.9 us
    reduce_sum x3, other arithmetic, from_root(): return jnp.sum(lax.all_gather(block, axis), axis=0)  30.2 us
  transfers between devices with their start and end apart: 4, of which 4 were waited for; matrix products, arithmetic and copies ran while one was open for 2% of the time, Pallas kernels for 0%

profile of v1, /device:TPU:0, one launch (start us, length us, event | category | flops | bytes accessed | tf_op | source)
XLA Modules:
  0.0 1281.3 jit_solution(18398562320239206646)
XLA Ops:
  6.5 14.5 %reshape_squeeze.3 = bf16[4,1,512,4,512]{4,3,2,0,1:T(4,128)(2,1)} reshape(bf16[1,2048,2048]{2,1,0:T(8,128)(2,1)} %param.5) | data formatting | bytes 16777216 | tf_op jit(solution)/shard_map/reshape;squeeze | solution.py:23
  21.0 98.5 %all_to_all.10 = bf16[4,1,512,4,512]{4,3,2,1,0:T(4,128)(2,1)S(1)} all-to-all(bf16[4,1,512,4,512]{4,3,2,1,0:T(4,128)(2,1)} %bitcast.92), channel_id=1, replica_groups=mesh['frow'=4,'fcol'=2,'sub'=4] {'frow'}, dimensions={0} | all-to-all | bytes 16777216 | tf_op jit(solution)/shard_map/all_to_all | solution.py:36
  119.5 20.9 %copy.40 = bf16[4,1,512,4,512]{4,0,2,1,3:T(4,128)(2,1)} copy(bf16[4,1,512,4,512]{4,3,2,1,0:T(4,128)(2,1)S(1)} %all_to_all.10) | data formatting | bytes 16777216 | tf_op jit(solution)/shard_map/all_to_all | solution.py:36
  140.3 5.8 all-to-all-start.1
  146.2 0.6 fusion.61
  152.4 0.2 maximum_reduce_fusion
  152.8 0.7 gather_fusion
  153.7 0.2 compare_reduce_fusion
  154.0 174.5 %all-to-all-done.1 = bf16[4,1,512,4,512]{4,0,2,1,3:T(4,128)(2,1)} async-done(((bf16[4,1,512,4,512]{4,0,2,1,3:T(4,128)(2,1)}), bf16[4,1,512,4,512]{4,0,2,1,3:T(4,128)(2,1)}, u32[]{:S(2)}, u32[]{:S(2)}) %all-to-all-start.1) | async-done | bytes 8388640 | tf_op jit(solution)/shard_map/all_to_all | solution.py:35
  328.5 11.5 convolution_bitcast_fusion
  340.0 4.5 fusion.3
  344.5 21.7 %dynamic_update_slice.4 = f32[16,512,512]{2,0,1:T(8,128)} dynamic-update-slice(f32[16,512,512]{2,0,1:T(8,128)} %convolution_bitcast_fusion, f32[1,512,512]{2,0,1:T(1,128)S(1)} %fusion.3, s32[]{:T(128)S(6)} %min.4, s32[]{:T(128)} %constant.231.clone.1, s32[]{:T(128)} %constant.231.clone.1) | dynamic-update-slice | bytes 2097156 | tf_op jit(solution)/shard_map/jit(dynamic_update_index_in_dim)/dynamic_update_slice | solution.py:51
  366.2 4.5 broadcast_select_fusion.1
  370.7 0.9 copy.43
  371.6 0.5 all-gather.9.cloned.1.call-start
  372.4 17.7 %copy.42 = f32[16,512,512]{2,1,0:T(8,128)} copy(f32[16,512,512]{2,0,1:T(8,128)} %dynamic_update_slice.4) | data formatting | bytes 33554432 | tf_op jit(solution)/shard_map/jit(dynamic_update_index_in_dim)/dynamic_update_slice | solution.py:51
  390.1 14.8 %all-gather.5.cloned.1.call-done = bf16[4,512,512]{2,1,0:T(8,128)(2,1)} async-done(((bf16[1,512,512]{2,1,0:T(8,128)(2,1)}), bf16[4,512,512]{2,1,0:T(8,128)(2,1)}) %all-gather.5.cloned.1.call-update) | async-done | bytes 2097168 | tf_op jit(solution)/shard_map/all_gather | solution.py:12
  404.9 2.2 reduce_sum.36
  407.7 1.0 copy-done.1
  408.7 11.7 cholesky.103
  420.6 9.8 custom-call.30
  430.4 1.2 constant_dynamic-update-slice_fusion
  431.7 1.3 convolution_subtract_fusion.3
  432.9 11.7 cholesky.215
  444.7 10.0 custom-call.31
  454.7 0.3 convolution_dynamic-update-slice_fusion
  454.9 1.3 convolution_subtract_fusion.4
  456.2 11.7 cholesky.236
  468.0 0.6 compare_reduce_fusion.2
  468.6 9.8 custom-call.32
  478.6 1.2 convolution_subtract_fusion.5
  479.9 11.9 cholesky.253
  491.8 0.6 compare_reduce_fusion.1
  492.4 0.7 compare_reduce_fusion.3
  495.6 1.1 select_select_fusion
  496.7 11.7 while.1
  496.8 0.6 fusion.69
  497.4 2.2 bitcast_dynamic-update-slice_fusion.2
  499.7 0.6 fusion.69
  500.3 2.2 bitcast_dynamic-update-slice_fusion.2
  502.6 0.6 fusion.69
  503.2 2.2 bitcast_dynamic-update-slice_fusion.2
  505.6 0.6 fusion.69
  506.2 2.2 bitcast_dynamic-update-slice_fusion.2
  508.4 39.3 %custom-call.33 = f32[4,128,128]{1,2,0:T(8,128)S(1)} custom-call(f32[4,128,128]{2,1,0:T(8,128)S(1)} %get-tuple-element.12), custom_call_target="InvertDiagBlocksLowerTriangular" | custom-call | tf_op jit(solution)/shard_map/triangular_solve | solution.py:60
  547.7 0.3 fusion.25
  548.0 1.2 convolution_subtract_fusion.1
  549.2 0.4 fusion.37
  549.7 1.3 convolution_subtract_fusion
  551.0 0.4 fusion.35
  551.4 1.6 convolution_subtract_fusion.2
  553.0 0.4 fusion.34
  553.4 31.9 %convert_select_fusion = (bf16[8192,512]{1,0:T(8,128)(2,1)}, f32[8192,512]{1,0:T(8,128)}) fusion(pred[]{:T(512)S(6)} %eq.66, f32[8192,512]{1,0:T(8,128)} %bitcast.89, f32[128,512]{1,0:T(8,128)S(1)} %fusion.34, f32[128,512]{1,0:T(8,128)S(1)} %fusion.35, f32[128,512]{1,0:T(8,128)S(1)} %fusion.37, f32[128,512]{1,0:T(8,128)S(1)} %fusion.25), kind=kOutput, calls=%fused_computation.8 | convolution fusion | flops 25778978816 | bytes 42991616 | tf_op jit(solution)/shard_map/dot_general | solution.py:61
  585.3 0.4 all-gather.7.cloned.1.call-start
  585.8 563.6 %all-gather.9.cloned.1.call-done = bf16[65536,512]{1,0:T(8,128)(2,1)} async-done(((bf16[8192,512]{1,0:T(8,128)(2,1)}), bf16[65536,512]{1,0:T(8,128)(2,1)}) %all-gather.9.cloned.1.call-update) | async-done | bytes 67108880 | tf_op jit(solution)/shard_map/all_gather | solution.py:12
  1149.5 25.8 %reduce_sum.37 = bf16[8192,512]{1,0:T(8,128)(2,1)} reduce(bf16[8,8192,512]{2,1,0:T(8,128)(2,1)} %bitcast.25, bf16[]{:T(256)} %constant.239.clone.1), dimensions={0}, to_apply=%region_9.10 | reduce | flops 29360128 | bytes 75497472 | tf_op jit(solution)/shard_map/reduce_sum | solution.py:12
  1175.3 11.4 copy.47
  1186.6 3.5 broadcast_select_fusion
  1190.2 0.9 copy.48
  1191.1 33.5 %all-gather.7.cloned.1.call-done = bf16[4,512,512]{2,1,0:T(8,128)(2,1)} async-done(((bf16[1,512,512]{2,1,0:T(8,128)(2,1)}), bf16[4,512,512]{2,1,0:T(8,128)(2,1)}) %all-gather.7.cloned.1.call-update) | async-done | bytes 2097168 | tf_op jit(solution)/shard_map/all_gather | solution.py:12
  1224.6 2.2 reduce_sum.38
  1226.8 19.7 %multiply_subtract_fusion = f32[16,512,512]{2,0,1:T(8,128)} fusion(f32[16,512,512]{2,0,1:T(8,128)} %dynamic_update_slice.4, f32[16]{0:T(128)S(1)} %convert_bitcast_fusion, bf16[512,512]{1,0:T(8,128)(2,1)S(1)} %reduce_sum.38, bf16[16,512,512]{2,1,0:T(8,128)(2,1)} %bitcast.91), kind=kOutput, calls=%fused_computation.4 | convolution fusion | flops 4303355904 | bytes 42467392 | tf_op jit(solution)/shard_map/ra,ba->rb/dot_general | solution.py:75
  1246.5 15.2 %copy.50 = f32[16,512,512]{2,1,0:T(8,128)S(1)} copy(f32[16,512,512]{2,0,1:T(8,128)} %multiply_subtract_fusion) | data formatting | bytes 33554432 | tf_op jit(solution)/shard_map/sub | solution.py:78
  1261.7 12.8 %bitcast_select_fusion = f32[8192,512]{1,0:T(8,128)} fusion(f32[8192,512]{1,0:T(8,128)} %get-tuple-element.38, f32[16,512,512]{2,1,0:T(8,128)S(1)} %copy.50, pred[]{:T(512)S(6)} %eq.66), kind=kLoop, calls=%fused_computation.3 | loop fusion | flops 4194304 | bytes 50331648 | tf_op jit(solution)/shard_map/jit(_where)/select_n | solution.py:80
  (46 shorter events, 2.3 us)
Async XLA Ops:
  140.3 5.9 copy-start
  140.3 11.9 copy-start.3
  140.3 13.4 %copy-start.2 = (f32[8192]{0:T(1024)S(1)}, f32[8192]{0:T(1024)}, u32[]{:S(2)}) copy-start(f32[8192]{0:T(1024)} %param.8) | copy-start | bytes 98308
  140.3 188.2 %all-to-all-start.1 = ((bf16[4,1,512,4,512]{4,0,2,1,3:T(4,128)(2,1)}), bf16[4,1,512,4,512]{4,0,2,1,3:T(4,128)(2,1)}, u32[]{:S(2)}, u32[]{:S(2)}) async-start(bf16[4,1,512,4,512]{4,0,2,1,3:T(4,128)(2,1)} %copy.40), calls=%async_computation.1 | async-start | bytes 16777216 | tf_op jit(solution)/shard_map/all_to_all | solution.py:35
  146.1 258.8 %all-gather.5.cloned.1.call-start = ((), (), s32[]{:S(2)}) async-start(), calls=%async_computation.2 | async-start | bytes 2621440 | tf_op jit(solution)/shard_map/all_gather | solution.py:12
  371.6 777.8 %all-gather.9.cloned.1.call-start = ((), (), s32[]{:S(2)}) async-start(), calls=%async_computation.4 | async-start | bytes 75497472 | tf_op jit(solution)/shard_map/all_gather | solution.py:12
  407.7 1.0 copy-start.1
  585.3 639.3 %all-gather.7.cloned.1.call-start = ((), (), s32[]{:S(2)}) async-start(), calls=%async_computation.3 | async-start | bytes 2621440 | tf_op jit(solution)/shard_map/all_gather | solution.py:12
  1175.3 15.8 %copy-start.4 = (s32[16,1]{0,1:T(1,128)S(1)}, s32[16,1]{0,1:T(1,128)}, u32[]{:S(2)}) copy-start(s32[16,1]{0,1:T(1,128)} %param.9) | copy-start | bytes 196
Sparse Core Ops, SparseCore 0:
  371.8 33.0 all-gather.4
  585.5 563.9 all-gather.8
  1191.2 33.3 all-gather.6
